TPU v7x, 128 devices: a whole 4x4x4 slice. The times are simulated.
128 devices in a mesh: rep: 32 (over y, z, x_lo), grp: 4 (over x_hi, core).
Axes of the slice: x: 4 (x_hi: 2, x_lo: 2; x = x_hi * 2 + x_lo), y: 4, z: 4, core: 2. Of those that a mesh axis runs over, the one named last changes fastest.
Arguments:
- tokens: bfloat16 [64, 1024, 768], P('rep', 'grp'), may hold values from -6 to 6
- segment: int32 [64, 1024], P('rep'), may hold values from 0 to 1, as said below
- piece_start: int32 [64, 1024], P('rep'), may hold values from 0 to 1023, as said below
- w_query: bfloat16 [768, 768], P('grp'), may hold values from -0.21875 to 0.21875
- w_key: bfloat16 [768, 768], P('grp'), may hold values from -0.21875 to 0.21875
- w_value: bfloat16 [768, 768], P('grp'), may hold values from -0.21875 to 0.21875
- w_out: bfloat16 [768, 768], P('grp'), may hold values from -3.5 to 3.5
- w_gate: bfloat16 [768, 3072], P('grp'), may hold values from -0.21875 to 0.21875
- w_up: bfloat16 [768, 3072], P('grp'), may hold values from -0.21875 to 0.21875
- w_down: bfloat16 [3072, 768], P('grp'), may hold values from -0.109375 to 0.109375
- cotangent: bfloat16 [64, 1024, 768], P('rep', 'grp'), may hold values from -6 to 6
Outputs:
- output: bfloat16 [64, 1024, 768], P('rep', 'grp')
- grad_tokens: bfloat16 [64, 1024, 768], P('rep', 'grp')
- grad_query: float32 [768, 768], P('grp')
- grad_key: float32 [768, 768], P('grp')
- grad_value: float32 [768, 768], P('grp')
- grad_out: float32 [768, 768], P('grp')
- grad_gate: float32 [768, 3072], P('grp')
- grad_up: float32 [768, 3072], P('grp')
- grad_down: float32 [3072, 768], P('grp')
Inputs may be any that keep to these rules, and one draw needn't show every extreme that they name: `segment`: along a sequence the numbers start at 0, never fall, rise by one at a time, and rise only at the first position of a picture piece. `piece_start`: each sequence holds 2 picture pieces of 256 positions, the k-th lying within positions k * (512) to (k + 1) * 512 - 1; a piece's positions hold its first position, all other positions their own.
All inputs are finite; a program needn't handle non-finite values.
Results may differ from a plain program's by a relative error of at most 0.029.
Values may be sent and summed in bfloat16 or wider, within the bound.
No kernel may reach another device: no remote copies, remote signals or barrier semaphores. Data moves between devices by JAX's collectives and lax.ppermute only.
A program may use at most 256 MiB of HBM per device.

v0:
```python
import jax
import jax.numpy as jnp
from jax import lax
from jax.sharding import PartitionSpec as P

HEADS = 12
HDIM = 64


def layer_norm(hidden):
    centred = hidden - jnp.mean(hidden, axis=-1, keepdims=True)
    spread = jnp.mean(centred * centred, axis=-1, keepdims=True)
    return centred * lax.rsqrt(spread + 1e-05)


def rotate(heads, cosine, sine):
    half = heads.shape[-1] // 2
    first = heads[..., :half]
    second = heads[..., half:]
    return jnp.concatenate(
        [first * cosine - second * sine, second * cosine + first * sine], axis=-1
    )


def gated(gate, upper):
    return gate / (1.0 + jnp.exp(-gate)) * upper


def matmul(left, right):
    return jnp.dot(left, right, preferred_element_type=jnp.float32)


def contract_rows(left, right):
    return lax.dot_general(
        left, right, (((0,), (0,)), ((), ())), preferred_element_type=jnp.float32
    )


def contract_cols(left, right):
    return lax.dot_general(
        left, right, (((1,), (1,)), ((), ())), preferred_element_type=jnp.float32
    )


def body(
    tokens, segment, piece_start, w_query, w_key, w_value, w_out, w_gate, w_up, w_down, cotangent
):
    local_length = tokens.shape[1]
    groups = lax.axis_size("grp")
    full_length = local_length * groups
    width = tokens.shape[2]
    head_count = HEADS
    head_size = HDIM
    scale = head_size ** (-0.5)
    first_row = lax.axis_index("grp") * local_length
    rows = first_row + jnp.arange(local_length, dtype=jnp.int32)
    columns = jnp.arange(full_length, dtype=jnp.int32)
    inverse = 10000.0 ** (-jnp.arange(0, head_size, 2).astype(jnp.float32) / head_size)
    angles = rows.astype(jnp.float32)[:, None] * inverse[None, :]
    cosine = jnp.cos(angles)[:, None, :]
    sine = jnp.sin(angles)[:, None, :]
    shards = (w_query, w_key, w_value, w_out, w_gate, w_up, w_down)
    totals = [jnp.zeros((shard.shape[0] * groups, shard.shape[1]), jnp.float32) for shard in shards]
    outputs = []
    input_grads = []
    for index in range(tokens.shape[0]):
        full = (
            lax.all_gather(w_query, "grp", axis=0, tiled=True),
            lax.all_gather(w_key, "grp", axis=0, tiled=True),
            lax.all_gather(w_value, "grp", axis=0, tiled=True),
            lax.all_gather(w_out, "grp", axis=0, tiled=True),
            lax.all_gather(w_gate, "grp", axis=0, tiled=True),
            lax.all_gather(w_up, "grp", axis=0, tiled=True),
            lax.all_gather(w_down, "grp", axis=0, tiled=True),
        )
        query_weight, key_weight, value_weight, out_weight, gate_weight, up_weight, down_weight = (
            full
        )
        hidden = tokens[index].astype(jnp.float32)
        normed, norm_one_back = jax.vjp(layer_norm, hidden)
        normed_low = normed.astype(jnp.bfloat16)
        query_heads = rotate(
            matmul(normed_low, query_weight).reshape(local_length, head_count, head_size),
            cosine,
            sine,
        ).astype(jnp.bfloat16)
        keys = (
            rotate(
                matmul(normed_low, key_weight).reshape(local_length, head_count, head_size),
                cosine,
                sine,
            )
            .reshape(local_length, width)
            .astype(jnp.bfloat16)
        )
        values = matmul(normed_low, value_weight).astype(jnp.bfloat16)
        all_keys, all_values = (
            lax.all_gather(keys, "grp", axis=0, tiled=True),
            lax.all_gather(values, "grp", axis=0, tiled=True),
        )
        key_heads = all_keys.reshape(full_length, head_count, head_size)
        value_heads = all_values.reshape(full_length, head_count, head_size)
        seg_row = segment[index]
        start_row = piece_start[index]
        seg_local = lax.dynamic_slice_in_dim(seg_row, first_row, local_length)
        start_local = lax.dynamic_slice_in_dim(start_row, first_row, local_length)
        causal = columns[None, :] <= rows[:, None]
        same_piece = start_local[:, None] == start_row[None, :]
        allowed = (seg_local[:, None] == seg_row[None, :]) & (causal | same_piece)

        def scores_of(heads_in):
            raw = jnp.einsum(
                "qhd,khd->hqk", heads_in, key_heads, preferred_element_type=jnp.float32
            )
            return jnp.where(allowed[None], raw * scale, -1e30)

        scores = scores_of(query_heads)
        highest = jnp.max(scores, axis=-1, keepdims=True)
        expd = jnp.exp(scores - highest)
        total = jnp.sum(expd, axis=-1, keepdims=True)
        log_total = highest + jnp.log(total)
        probs_low = (expd / total).astype(jnp.bfloat16)
        mixed = jnp.einsum(
            "hqk,khd->qhd", probs_low, value_heads, preferred_element_type=jnp.float32
        )
        mixed_low = mixed.reshape(local_length, width).astype(jnp.bfloat16)
        after = hidden + matmul(mixed_low, out_weight)
        normed_two, norm_two_back = jax.vjp(layer_norm, after)
        normed_two_low = normed_two.astype(jnp.bfloat16)
        gate = matmul(normed_two_low, gate_weight)
        upper = matmul(normed_two_low, up_weight)
        active, gate_back = jax.vjp(gated, gate, upper)
        active_low = active.astype(jnp.bfloat16)
        result = after + matmul(active_low, down_weight)
        outputs.append(result.astype(jnp.bfloat16))
        full = (
            lax.all_gather(w_query, "grp", axis=0, tiled=True),
            lax.all_gather(w_key, "grp", axis=0, tiled=True),
            lax.all_gather(w_value, "grp", axis=0, tiled=True),
            lax.all_gather(w_out, "grp", axis=0, tiled=True),
            lax.all_gather(w_gate, "grp", axis=0, tiled=True),
            lax.all_gather(w_up, "grp", axis=0, tiled=True),
            lax.all_gather(w_down, "grp", axis=0, tiled=True),
        )
        query_weight, key_weight, value_weight, out_weight, gate_weight, up_weight, down_weight = (
            full
        )
        grad_result = cotangent[index]
        totals[6] = totals[6] + contract_rows(active_low, grad_result)
        grad_active = contract_cols(grad_result, down_weight)
        grad_gate, grad_upper = gate_back(grad_active)
        gate_low = grad_gate.astype(jnp.bfloat16)
        upper_low = grad_upper.astype(jnp.bfloat16)
        totals[4] = totals[4] + contract_rows(normed_two_low, gate_low)
        totals[5] = totals[5] + contract_rows(normed_two_low, upper_low)
        grad_normed_two = contract_cols(gate_low, gate_weight) + contract_cols(upper_low, up_weight)
        grad_after = grad_result.astype(jnp.float32) + norm_two_back(grad_normed_two)[0]
        after_low = grad_after.astype(jnp.bfloat16)
        totals[3] = totals[3] + contract_rows(mixed_low, after_low)
        grad_mixed = (
            contract_cols(after_low, out_weight)
            .astype(jnp.bfloat16)
            .reshape(local_length, head_count, head_size)
        )
        probs = jnp.exp(scores_of(query_heads) - log_total)
        grad_probs = jnp.einsum(
            "qhd,khd->hqk", grad_mixed, value_heads, preferred_element_type=jnp.float32
        )
        inner = jnp.sum(probs * grad_probs, axis=-1, keepdims=True)
        grad_raw = (probs * (grad_probs - inner) * scale).astype(jnp.bfloat16)
        grad_query = jnp.einsum(
            "hqk,khd->qhd", grad_raw, key_heads, preferred_element_type=jnp.float32
        )
        again_low = probs.astype(jnp.bfloat16)
        grad_keys = jnp.einsum(
            "hqk,qhd->khd", grad_raw, query_heads, preferred_element_type=jnp.float32
        ).reshape(full_length, width)
        grad_values = jnp.einsum(
            "hqk,qhd->khd", again_low, grad_mixed, preferred_element_type=jnp.float32
        ).reshape(full_length, width)
        own_keys, own_values = (
            lax.psum_scatter(
                grad_keys.astype(jnp.bfloat16), "grp", scatter_dimension=0, tiled=True
            ).astype(jnp.float32),
            lax.psum_scatter(
                grad_values.astype(jnp.bfloat16), "grp", scatter_dimension=0, tiled=True
            ).astype(jnp.float32),
        )
        query_low = (
            rotate(grad_query, cosine, -sine).reshape(local_length, width).astype(jnp.bfloat16)
        )
        keys_low = (
            rotate(own_keys.reshape(local_length, head_count, head_size), cosine, -sine)
            .reshape(local_length, width)
            .astype(jnp.bfloat16)
        )
        values_low = own_values.astype(jnp.bfloat16)
        totals[0] = totals[0] + contract_rows(normed_low, query_low)
        totals[1] = totals[1] + contract_rows(normed_low, keys_low)
        totals[2] = totals[2] + contract_rows(normed_low, values_low)
        grad_normed = (
            contract_cols(query_low, query_weight)
            + contract_cols(keys_low, key_weight)
            + contract_cols(values_low, value_weight)
        )
        grad_hidden = grad_after + norm_one_back(grad_normed)[0]
        input_grads.append(grad_hidden.astype(jnp.bfloat16))
    owned = (
        lax.psum_scatter(
            totals[0].astype(jnp.bfloat16), "grp", scatter_dimension=0, tiled=True
        ).astype(jnp.float32),
        lax.psum_scatter(
            totals[1].astype(jnp.bfloat16), "grp", scatter_dimension=0, tiled=True
        ).astype(jnp.float32),
        lax.psum_scatter(
            totals[2].astype(jnp.bfloat16), "grp", scatter_dimension=0, tiled=True
        ).astype(jnp.float32),
        lax.psum_scatter(
            totals[3].astype(jnp.bfloat16), "grp", scatter_dimension=0, tiled=True
        ).astype(jnp.float32),
        lax.psum_scatter(
            totals[4].astype(jnp.bfloat16), "grp", scatter_dimension=0, tiled=True
        ).astype(jnp.float32),
        lax.psum_scatter(
            totals[5].astype(jnp.bfloat16), "grp", scatter_dimension=0, tiled=True
        ).astype(jnp.float32),
        lax.psum_scatter(
            totals[6].astype(jnp.bfloat16), "grp", scatter_dimension=0, tiled=True
        ).astype(jnp.float32),
    )
    summed = (
        lax.psum(owned[0].astype(jnp.bfloat16), "rep").astype(jnp.float32),
        lax.psum(owned[1].astype(jnp.bfloat16), "rep").astype(jnp.float32),
        lax.psum(owned[2].astype(jnp.bfloat16), "rep").astype(jnp.float32),
        lax.psum(owned[3].astype(jnp.bfloat16), "rep").astype(jnp.float32),
        lax.psum(owned[4].astype(jnp.bfloat16), "rep").astype(jnp.float32),
        lax.psum(owned[5].astype(jnp.bfloat16), "rep").astype(jnp.float32),
        lax.psum(owned[6].astype(jnp.bfloat16), "rep").astype(jnp.float32),
    )
    return (
        jnp.stack(outputs),
        jnp.stack(input_grads),
        summed[0],
        summed[1],
        summed[2],
        summed[3],
        summed[4],
        summed[5],
        summed[6],
    )


def solution(mesh):
    placed = (
        P("rep", "grp", None),
        P("rep", None),
        P("rep", None),
        P("grp", None),
        P("grp", None),
        P("grp", None),
        P("grp", None),
        P("grp", None),
        P("grp", None),
        P("grp", None),
        P("rep", "grp", None),
    )
    return jax.shard_map(
        body,
        mesh=mesh,
        in_specs=placed,
        out_specs=(
            P("rep", "grp", None),
            P("rep", "grp", None),
            P("grp", None),
            P("grp", None),
            P("grp", None),
            P("grp", None),
            P("grp", None),
            P("grp", None),
            P("grp", None),
        ),
        check_vma=False,
    )
```

profile of v0, /device:TPU:0, one launch (start us, length us, event | category | flops | bytes accessed | tf_op | source)
XLA Modules:
  0.0 1195.9 jit_solution(17734370692806180140)
XLA Ops:
  13.2 20.5 %all-gather.18.cloned.1.call-done = bf16[768,768]{1,0:T(8,128)(2,1)} async-done(((bf16[192,768]{1,0:T(8,128)(2,1)}), bf16[768,768]{1,0:T(8,128)(2,1)}) %all-gather.18.cloned.1.call-update) | async-done | bytes 1179664 | tf_op jit(solution)/shard_map/all_gather | solution.py:69
  35.2 21.1 %all-gather.16.cloned.1.call-done = bf16[768,768]{1,0:T(8,128)(2,1)} async-done(((bf16[192,768]{1,0:T(8,128)(2,1)}), bf16[768,768]{1,0:T(8,128)(2,1)}) %all-gather.16.cloned.1.call-update) | async-done | bytes 1179664 | tf_op jit(solution)/shard_map/all_gather | solution.py:68
  62.5 16.5 %all-gather.12.cloned.1.call-done = bf16[768,768]{1,0:T(8,128)(2,1)} async-done(((bf16[192,768]{1,0:T(8,128)(2,1)}), bf16[768,768]{1,0:T(8,128)(2,1)}) %all-gather.12.cloned.1.call-update) | async-done | bytes 1179664 | tf_op jit(solution)/shard_map/all_gather | solution.py:70
  78.9 2.5 convolution_convert_fusion.2
  81.6 2.5 convolution_convert_fusion.3
  88.7 15.6 %all-gather.32.cloned.1.call-done = bf16[1024,768]{0,1:T(8,128)(2,1)} async-done(((bf16[256,768]{0,1:T(8,128)(2,1)}), bf16[1024,768]{0,1:T(8,128)(2,1)}) %all-gather.32.cloned.1.call-update) | async-done | bytes 1572880 | tf_op jit(solution)/shard_map/all_gather | solution.py:98
  104.4 3.7 fusion.7
  108.1 4.6 copy-done.1
  112.7 3.8 fusion.5
  116.5 13.1 %all-gather.30.cloned.1.call-done = bf16[1024,768]{1,0:T(8,128)(2,1)} async-done(((bf16[256,768]{1,0:T(8,128)(2,1)}), bf16[1024,768]{1,0:T(8,128)(2,1)}) %all-gather.30.cloned.1.call-update) | async-done | bytes 1572880 | tf_op jit(solution)/shard_map/all_gather | solution.py:99
  129.6 1.7 copy.33
  131.4 7.0 fusion.86
  138.4 16.5 %all-gather.14.cloned.1.call-done = bf16[1024,768]{1,0:T(8,128)(2,1)} async-done(((bf16[256,768]{1,0:T(8,128)(2,1)}), bf16[1024,768]{1,0:T(8,128)(2,1)}) %all-gather.14.cloned.1.call-update) | async-done | bytes 1572880 | tf_op jit(solution)/shard_map/all_gather | solution.py:99
  154.9 2.6 copy.30
  157.5 20.0 %all-gather.22.cloned.1.call-done = bf16[768,768]{1,0:T(8,128)(2,1)} async-done(((bf16[192,768]{1,0:T(8,128)(2,1)}), bf16[768,768]{1,0:T(8,128)(2,1)}) %all-gather.22.cloned.1.call-update) | async-done | bytes 1179664 | tf_op jit(solution)/shard_map/all_gather | solution.py:71
  177.5 1.8 fusion.202
  180.2 22.9 %all-gather.20.cloned.1.call-done = bf16[1024,768]{0,1:T(8,128)(2,1)} async-done(((bf16[256,768]{0,1:T(8,128)(2,1)}), bf16[1024,768]{0,1:T(8,128)(2,1)}) %all-gather.20.cloned.1.call-update) | async-done | bytes 1572880 | tf_op jit(solution)/shard_map/all_gather | solution.py:98
  203.1 3.7 fusion.6
  206.8 3.7 fusion.4
  211.6 4.3 fusion.87
  220.0 25.7 %all-gather.26.cloned.1.call-done = bf16[768,3072]{1,0:T(8,128)(2,1)} async-done(((bf16[192,3072]{1,0:T(8,128)(2,1)}), bf16[768,3072]{1,0:T(8,128)(2,1)}) %all-gather.26.cloned.1.call-update) | async-done | bytes 4718608 | tf_op jit(solution)/shard_map/all_gather | solution.py:73
  245.7 5.5 fusion.207
  251.3 36.9 %all-gather.24.cloned.1.call-done = bf16[768,3072]{1,0:T(8,128)(2,1)} async-done(((bf16[192,3072]{1,0:T(8,128)(2,1)}), bf16[768,3072]{1,0:T(8,128)(2,1)}) %all-gather.24.cloned.1.call-update) | async-done | bytes 4718608 | tf_op jit(solution)/shard_map/all_gather | solution.py:72
  288.2 5.5 fusion.206
  293.7 37.1 %all-gather.28.cloned.1.call-done = bf16[3072,768]{1,0:T(8,128)(2,1)} async-done(((bf16[768,768]{1,0:T(8,128)(2,1)}), bf16[3072,768]{1,0:T(8,128)(2,1)}) %all-gather.28.cloned.1.call-update) | async-done | bytes 4718608 | tf_op jit(solution)/shard_map/all_gather | solution.py:74
  330.8 8.3 multiply_convert_fusion.2
  340.7 1.7 slice-done.2
  346.1 3.1 fusion.204
  349.2 5.5 multiply_convert_fusion.3
  361.3 1.9 copy.34
  363.2 9.1 fusion.66
  373.7 2.2 convolution_convert_fusion
  377.1 8.4 fusion.69
  385.8 7.8 fusion.209
  393.6 34.9 %fusion.75 = bf16[12,64,1024]{2,1,0:T(8,128)(2,1)} fusion(f32[12,256,1024]{2,1,0:T(8,128)} %fusion.209, f32[12,256,1024]{2,1,0:T(8,128)} %copy-done.2, f32[12,256]{1,0:T(8,128)S(1)} %copy-done.71, pred[256,1024]{1,0:T(8,128)(4,1)} %copy-done.32, bf16[256,12,32]{0,2,1:T(8,128)(2,1)S(1)} %copy-done.55, bf16[256,12,32]{0,2,1:T(8,128)(2,1)S(1)} %copy-done.53), kind=kOutput, calls=%fused_computation.68 | convolution fusion | flops 438833152 | bytes 27406336 | tf_op jit(solution)/shard_map/hqk,qhd->khd/dot_general | solution.py:175
  429.0 7.8 fusion.212
  436.9 34.6 %fusion.72 = bf16[12,64,1024]{2,1,0:T(8,128)(2,1)} fusion(f32[12,256,1024]{2,1,0:T(8,128)} %fusion.212, f32[12,256,1024]{2,1,0:T(8,128)} %copy-done.1, f32[12,256]{1,0:T(8,128)S(1)} %copy-done.73, pred[256,1024]{1,0:T(8,128)(4,1)} %copy-done.31, bf16[256,12,32]{0,2,1:T(8,128)(2,1)S(1)} %copy-done.49, bf16[256,12,32]{0,2,1:T(8,128)(2,1)S(1)} %copy-done.51), kind=kOutput, calls=%fused_computation.67 | convolution fusion | flops 438833152 | bytes 27406336 | tf_op jit(solution)/shard_map/hqk,qhd->khd/dot_general | solution.py:175
  474.8 3.1 fusion.183
  477.9 3.5 add_convert_fusion.6
  481.7 34.6 %fusion.81 = f32[256,12,64]{0,2,1:T(8,128)} fusion(bf16[1024,12,64]{0,2,1:T(8,128)(2,1)} %bitcast.263, f32[12,256,1024]{2,1,0:T(8,128)} %fusion.209, f32[12,256,1024]{2,1,0:T(8,128)} %copy-done.2, f32[12,256]{1,0:T(8,128)S(1)} %copy-done.72, pred[256,1024]{1,0:T(8,128)(4,1)} %copy-done.32), kind=kOutput, calls=%fused_computation.70 | convolution fusion | flops 437260288 | bytes 27799552 | tf_op jit(solution)/shard_map/hqk,khd->qhd/dot_general | solution.py:171
  516.2 34.3 %fusion.78 = f32[256,12,64]{0,2,1:T(8,128)} fusion(bf16[1024,12,64]{0,2,1:T(8,128)(2,1)} %bitcast.261, f32[12,256,1024]{2,1,0:T(8,128)} %fusion.212, f32[12,256,1024]{2,1,0:T(8,128)} %copy-done.1, f32[12,256]{1,0:T(8,128)S(1)} %copy-done.74, pred[256,1024]{1,0:T(8,128)(4,1)} %copy-done.31), kind=kOutput, calls=%fused_computation.69 | convolution fusion | flops 437260288 | bytes 27799552 | tf_op jit(solution)/shard_map/hqk,khd->qhd/dot_general | solution.py:171
  552.8 2.6 multiply_subtract_fusion
  557.0 1.7 add_convert_fusion.7
  560.9 1.7 add_convert_fusion.8
  562.7 3.0 fusion.121
  565.7 3.6 add_convert_fusion
  570.3 3.0 fusion.216
  573.3 3.7 add_convert_fusion.1
  577.1 3.1 fusion.215
  580.2 3.7 add_convert_fusion.2
  584.2 4.3 reduce-scatter.24.cloned.1.call-done
  588.6 34.6 %reduce-scatter.22.cloned.1.call-done = bf16[192,768]{1,0:T(8,128)(2,1)} async-done(((bf16[768,768]{1,0:T(8,128)(2,1)}), bf16[192,768]{1,0:T(8,128)(2,1)}) %reduce-scatter.22.cloned.1.call-update) | async-done | bytes 294928 | tf_op jit(solution)/shard_map/reduce_scatter | solution.py:212
  623.2 35.5 %reduce-scatter.20.cloned.1.call-done = bf16[192,768]{1,0:T(8,128)(2,1)} async-done(((bf16[768,768]{1,0:T(8,128)(2,1)}), bf16[192,768]{1,0:T(8,128)(2,1)}) %reduce-scatter.20.cloned.1.call-update) | async-done | bytes 294928 | tf_op jit(solution)/shard_map/reduce_scatter | solution.py:209
  658.7 56.7 %reduce-scatter.32.cloned.1.call-done = bf16[768,768]{1,0:T(8,128)(2,1)} async-done(((bf16[3072,768]{1,0:T(8,128)(2,1)}), bf16[768,768]{1,0:T(8,128)(2,1)}) %reduce-scatter.32.cloned.1.call-update) | async-done | bytes 1179664 | tf_op jit(solution)/shard_map/reduce_scatter | solution.py:227
  715.4 57.1 %reduce-scatter.30.cloned.1.call-done = bf16[192,3072]{1,0:T(8,128)(2,1)} async-done(((bf16[768,3072]{1,0:T(8,128)(2,1)}), bf16[192,3072]{1,0:T(8,128)(2,1)}) %reduce-scatter.30.cloned.1.call-update) | async-done | bytes 1179664 | tf_op jit(solution)/shard_map/reduce_scatter | solution.py:224
  772.5 56.9 %reduce-scatter.28.cloned.1.call-done = bf16[192,3072]{1,0:T(8,128)(2,1)} async-done(((bf16[768,3072]{1,0:T(8,128)(2,1)}), bf16[192,3072]{1,0:T(8,128)(2,1)}) %reduce-scatter.28.cloned.1.call-update) | async-done | bytes 1179664 | tf_op jit(solution)/shard_map/reduce_scatter | solution.py:221
  829.4 4.3 fusion.88
  833.7 3.9 fusion.89
  844.6 330.8 %all-reduce.3.cloned.1.call-done = (bf16[192,768]{1,0:T(8,128)(2,1)}, bf16[192,768]{1,0:T(8,128)(2,1)}, bf16[192,768]{1,0:T(8,128)(2,1)}, bf16[192,768]{1,0:T(8,...) async-done(((bf16[192,768]{1,0:T(8,128)(2,1)}, bf16[192,768]{1,0:T(8,128)(2,1)}, bf16[192,768]{1,0:T(8,128)(2,1)}, ...) | async-done | bytes 4718608 | tf_op jit(solution)/shard_map/psum | solution.py:232
  1175.3 1.9 convert_element_type.379
  1177.2 1.9 convert_element_type.381
  1179.2 1.8 convert_element_type.383
  1181.0 1.8 convert_element_type.385
  1182.8 2.9 convert_element_type.387
  (320 shorter events, 59.6 us)
Async XLA Ops:
  7.2 50.7 %copy-start = (bf16[2,256,768]{2,1,0:T(8,128)(2,1)S(1)}, bf16[2,256,768]{2,1,0:T(8,128)(2,1)}, u32[]{:S(2)}) copy-start(bf16[2,256,768]{2,1,0:T(8,128)(2,1)} %param.11) | copy-start | bytes 2359300
  7.2 26.5 %all-gather.18.cloned.1.call-start = ((), (), s32[]{:S(2)}) async-start(), calls=%async_computation.14 | async-start | bytes 1474560 | tf_op jit(solution)/shard_map/all_gather | solution.py:69
  7.9 48.4 %all-gather.16.cloned.1.call-start = ((), (), s32[]{:S(2)}) async-start(), calls=%async_computation.13 | async-start | bytes 1474560 | tf_op jit(solution)/shard_map/all_gather | solution.py:68
  8.7 70.3 %all-gather.12.cloned.1.call-start = ((), (), s32[]{:S(2)}) async-start(), calls=%async_computation.11 | async-start | bytes 1474560 | tf_op jit(solution)/shard_map/all_gather | solution.py:70
  9.4 95.0 %all-gather.32.cloned.1.call-start = ((), (), s32[]{:S(2)}) async-start(), calls=%async_computation.21 | async-start | bytes 1966080 | tf_op jit(solution)/shard_map/all_gather | solution.py:98
  10.8 68.1 %copy-start.59 = (f32[256]{0:T(256)}, f32[256]{0:T(256)S(1)}, u32[]{:S(2)}) copy-start(f32[256]{0:T(256)S(1)} %get-tuple-element.88) | copy-start | bytes 3076
  10.8 70.8 %copy-start.57 = (f32[256]{0:T(256)}, f32[256]{0:T(256)S(1)}, u32[]{:S(2)}) copy-start(f32[256]{0:T(256)S(1)} %get-tuple-element.89) | copy-start | bytes 3076
  12.3 69.3 %copy-start.61 = (f32[256]{0:T(256)}, f32[256]{0:T(256)S(1)}, u32[]{:S(2)}) copy-start(f32[256]{0:T(256)S(1)} %fusion.146) | copy-start | bytes 3076
  13.1 47.1 %copy-start.56 = (f32[256,32]{0,1:T(8,128)}, f32[256,32]{0,1:T(8,128)S(1)}, u32[]{:S(2)}) copy-start(f32[256,32]{0,1:T(8,128)S(1)} %get-tuple-element.72) | copy-start | bytes 98308
  13.2 65.8 %copy-start.64 = (f32[256]{0:T(256)}, f32[256]{0:T(256)S(1)}, u32[]{:S(2)}) copy-start(f32[256]{0:T(256)S(1)} %fusion.148) | copy-start | bytes 3076
  61.6 42.8 %copy-start.48 = (bf16[256,12,32]{0,2,1:T(8,128)(2,1)}, bf16[256,12,32]{0,2,1:T(8,128)(2,1)S(1)}, u32[]{:S(2)}) copy-start(bf16[256,12,32]{0,2,1:T(8,128)(2,1)S(1)} %get-tuple-element.62) | copy-start | bytes 589828
  61.6 42.8 %copy-start.50 = (bf16[256,12,32]{0,2,1:T(8,128)(2,1)}, bf16[256,12,32]{0,2,1:T(8,128)(2,1)S(1)}, u32[]{:S(2)}) copy-start(bf16[256,12,32]{0,2,1:T(8,128)(2,1)S(1)} %get-tuple-element.63) | copy-start | bytes 589828
  62.4 67.2 %all-gather.30.cloned.1.call-start = ((), (), s32[]{:S(2)}) async-start(), calls=%async_computation.20 | async-start | bytes 1966080 | tf_op jit(solution)/shard_map/all_gather | solution.py:99
  81.5 6.4 copy-start.91
  81.5 6.4 copy-start.92
  81.5 73.4 %all-gather.14.cloned.1.call-start = ((), (), s32[]{:S(2)}) async-start(), calls=%async_computation.12 | async-start | bytes 1966080 | tf_op jit(solution)/shard_map/all_gather | solution.py:99
  84.2 93.4 %all-gather.22.cloned.1.call-start = ((), (), s32[]{:S(2)}) async-start(), calls=%async_computation.16 | async-start | bytes 1474560 | tf_op jit(solution)/shard_map/all_gather | solution.py:71
  84.9 118.2 %all-gather.20.cloned.1.call-start = ((), (), s32[]{:S(2)}) async-start(), calls=%async_computation.15 | async-start | bytes 1966080 | tf_op jit(solution)/shard_map/all_gather | solution.py:98
  85.8 160.0 %all-gather.26.cloned.1.call-start = ((), (), s32[]{:S(2)}) async-start(), calls=%async_computation.18 | async-start | bytes 5898240 | tf_op jit(solution)/shard_map/all_gather | solution.py:73
  86.5 201.7 %all-gather.24.cloned.1.call-start = ((), (), s32[]{:S(2)}) async-start(), calls=%async_computation.17 | async-start | bytes 5898240 | tf_op jit(solution)/shard_map/all_gather | solution.py:72
  87.1 243.8 %all-gather.28.cloned.1.call-start = ((), (), s32[]{:S(2)}) async-start(), calls=%async_computation.19 | async-start | bytes 5898240 | tf_op jit(solution)/shard_map/all_gather | solution.py:74
  87.8 387.0 %reduce-scatter.14.cloned.1.call-start = ((), (), s32[]{:S(2)}) async-start(), calls=%async_computation.23 | async-start | bytes 1966080 | tf_op jit(solution)/shard_map/reduce_scatter | solution.py:185
  88.7 42.7 %copy-start.31 = (pred[256,1024]{1,0:T(8,128)(4,1)}, pred[256,1024]{1,0:T(8,128)(4,1)S(1)}, u32[]{:S(2)}) copy-start(pred[256,1024]{1,0:T(8,128)(4,1)S(1)} %get-tuple-element.74) | copy-start | bytes 786436
  88.7 121.8 %copy-start.32 = (pred[256,1024]{1,0:T(8,128)(4,1)}, pred[256,1024]{1,0:T(8,128)(4,1)S(1)}, u32[]{:S(2)}) copy-start(pred[256,1024]{1,0:T(8,128)(4,1)S(1)} %get-tuple-element.73) | copy-start | bytes 786436
  116.5 21.9 %copy-start.63 = (f32[12,256]{1,0:T(8,128)}, f32[12,256]{1,0:T(8,128)S(1)}, u32[]{:S(2)}) copy-start(f32[12,256]{1,0:T(8,128)S(1)} %fusion.5) | copy-start | bytes 36868
  131.3 7.1 copy-start.12
  138.4 68.4 %copy-start.33 = (bf16[12,64,256]{2,1,0:T(8,128)(2,1)}, bf16[12,64,256]{2,1,0:T(8,128)(2,1)S(1)}, u32[]{:S(2)}) copy-start(bf16[12,64,256]{2,1,0:T(8,128)(2,1)S(1)} %fusion.86) | copy-start | bytes 1179652
  154.9 48.2 %copy-start.52 = (bf16[256,12,32]{0,2,1:T(8,128)(2,1)S(1)}, bf16[256,12,32]{0,2,1:T(8,128)(2,1)}, u32[]{:S(2)}) copy-start(bf16[256,12,32]{0,2,1:T(8,128)(2,1)} %get-tuple-element.44) | copy-start | bytes 589828
  154.9 48.2 %copy-start.54 = (bf16[256,12,32]{0,2,1:T(8,128)(2,1)S(1)}, bf16[256,12,32]{0,2,1:T(8,128)(2,1)}, u32[]{:S(2)}) copy-start(bf16[256,12,32]{0,2,1:T(8,128)(2,1)} %get-tuple-element.45) | copy-start | bytes 589828
  179.4 27.4 %copy-start.68 = (f32[256]{0:T(256)}, f32[256]{0:T(256)S(1)}, u32[]{:S(2)}) copy-start(f32[256]{0:T(256)S(1)} %broadcast_multiply_fusion) | copy-start | bytes 3076
  211.6 5.1 copy-start.3
  211.6 5.9 copy-start.89
  211.6 6.6 copy-start.69
  330.8 8.3 copy-start.93
  339.1 5.1 copy-start.42
  339.1 5.1 copy-start.44
  344.6 13.7 %copy-start.8 = (f32[256,768]{1,0:T(8,128)}, f32[256,768]{1,0:T(8,128)S(1)}, u32[]{:S(2)}) copy-start(f32[256,768]{1,0:T(8,128)S(1)} %get-tuple-element.25) | copy-start | bytes 2359300
  344.6 13.7 %copy-start.75 = (f32[256]{0:T(256)}, f32[256]{0:T(256)S(1)}, u32[]{:S(2)}) copy-start(f32[256]{0:T(256)S(1)} %negate_multiply_fusion.1) | copy-start | bytes 3076
  372.3 105.6 %reduce-scatter.18.cloned.1.call-start = ((), (), s32[]{:S(2)}) async-start(), calls=%async_computation.25 | async-start | bytes 1966080 | tf_op jit(solution)/shard_map/reduce_scatter | solution.py:185
  377.1 8.7 copy-start.40
  385.5 8.1 copy-start.53
  385.5 8.1 copy-start.55
  385.5 8.1 copy-start.71
  385.5 165.1 %reduce-scatter.12.cloned.1.call-start = ((), (), s32[]{:S(2)}) async-start(), calls=%async_computation.22 | async-start | bytes 1966080 | tf_op jit(solution)/shard_map/reduce_scatter | solution.py:182
  428.5 8.3 copy-start.49
  428.5 8.3 copy-start.51
  428.6 8.3 copy-start.73
  428.6 123.1 %reduce-scatter.16.cloned.1.call-start = ((), (), s32[]{:S(2)}) async-start(), calls=%async_computation.24 | async-start | bytes 1966080 | tf_op jit(solution)/shard_map/reduce_scatter | solution.py:182
  436.8 34.7 %copy-start.23 = (bf16[256,768]{1,0:T(8,128)(2,1)S(1)}, bf16[256,768]{1,0:T(8,128)(2,1)}, u32[]{:S(2)}) copy-start(bf16[256,768]{1,0:T(8,128)(2,1)} %copy-done.22) | copy-start | bytes 1179652
  471.5 112.7 %reduce-scatter.26.cloned.1.call-start = ((), (), s32[]{:S(2)}) async-start(), calls=%async_computation.29 | async-start | bytes 1474560 | tf_op jit(solution)/shard_map/reduce_scatter | solution.py:218
  474.7 7.0 copy-start.72
  474.7 113.9 %reduce-scatter.24.cloned.1.call-start = ((), (), s32[]{:S(2)}) async-start(), calls=%async_computation.28 | async-start | bytes 1474560 | tf_op jit(solution)/shard_map/reduce_scatter | solution.py:215
  481.4 34.8 %copy-start.74 = (f32[12,256]{1,0:T(8,128)S(1)}, f32[12,256]{1,0:T(8,128)}, u32[]{:S(2)}) copy-start(f32[12,256]{1,0:T(8,128)} %log_add_fusion) | copy-start | bytes 36868
  481.4 141.8 %reduce-scatter.22.cloned.1.call-start = ((), (), s32[]{:S(2)}) async-start(), calls=%async_computation.27 | async-start | bytes 1474560 | tf_op jit(solution)/shard_map/reduce_scatter | solution.py:212
  558.7 100.0 %reduce-scatter.20.cloned.1.call-start = ((), (), s32[]{:S(2)}) async-start(), calls=%async_computation.26 | async-start | bytes 1474560 | tf_op jit(solution)/shard_map/reduce_scatter | solution.py:209
  560.2 5.5 copy-start.19
  562.6 152.8 %reduce-scatter.32.cloned.1.call-start = ((), (), s32[]{:S(2)}) async-start(), calls=%async_computation.32 | async-start | bytes 5898240 | tf_op jit(solution)/shard_map/reduce_scatter | solution.py:227
  569.3 203.1 %reduce-scatter.30.cloned.1.call-start = ((), (), s32[]{:S(2)}) async-start(), calls=%async_computation.31 | async-start | bytes 5898240 | tf_op jit(solution)/shard_map/reduce_scatter | solution.py:224
  577.0 252.3 %reduce-scatter.28.cloned.1.call-start = ((), (), s32[]{:S(2)}) async-start(), calls=%async_computation.30 | async-start | bytes 5898240 | tf_op jit(solution)/shard_map/reduce_scatter | solution.py:221
  583.9 591.4 %all-reduce.3.cloned.1.call-start = ((), (), s32[]{:S(2)}) async-start(), calls=%async_computation.33 | async-start | bytes 9437184 | tf_op jit(solution)/shard_map/psum | solution.py:232
  833.7 4.9 copy-start.5
  833.7 5.4 copy-start.27
  1175.3 10.4 copy-start.47
  1177.2 10.1 copy-start.46
  (57 other events, 142.2 us)
Sparse Core Ops, SparseCore 0:
  9.7 23.9 all-gather.17
  35.3 20.9 all-gather.15
  58.0 20.9 all-gather.11
  81.0 23.2 all-gather.31
  106.5 23.1 all-gather.29
  131.7 23.1 all-gather.13
  156.5 20.9 all-gather.21
  179.7 23.2 all-gather.19
  204.8 40.9 all-gather.25
  247.2 40.9 all-gather.23
  289.9 40.9 all-gather.27
  372.4 34.5 reduce-scatter.13
  409.8 34.6 reduce-scatter.17
  447.0 34.6 reduce-scatter.11
  484.4 34.6 reduce-scatter.15
  521.6 32.2 reduce-scatter.25
  556.5 31.9 reduce-scatter.23
  591.1 32.0 reduce-scatter.21
  626.6 32.0 reduce-scatter.19
  661.2 54.1 reduce-scatter.31
  718.2 54.1 reduce-scatter.29
  775.1 54.1 reduce-scatter.27
  832.7 342.6 all-reduce.2
where the time goes:
time: 1200 us
  waiting for transfers between devices  827 us (69%)
  matrix products  285 us (24%)
  other arithmetic  44 us (4%)
  local copies, waits for them, and re-layouts  21.7 us (2%)
  between operations  16 us (1%)
    psum x1, waiting for transfers between devices, body(): lax.psum(owned[0].astype(jnp.bfloat16), 'rep').astype(jnp.float32)  331 us
    dot_general x2, matrix products, body(): jnp.einsum('hqk,qhd->khd', grad_raw, query_heads, preferred_element_type=...  69.5 us
    dot_general x2, matrix products, body(): jnp.einsum('hqk,khd->qhd', grad_raw, key_heads, preferred_element_type=jn...  68.9 us
    reduce_scatter x1, waiting for transfers between devices, body(): lax.psum_scatter(totals[5].astype(jnp.bfloat16), 'grp', scatter_dimension...  57.1 us
    reduce_scatter x1, waiting for transfers between devices, body(): lax.psum_scatter(totals[4].astype(jnp.bfloat16), 'grp', scatter_dimension...  56.9 us
    reduce_scatter x1, waiting for transfers between devices, body(): lax.psum_scatter(totals[6].astype(jnp.bfloat16), 'grp', scatter_dimension...  56.7 us
    all_gather x2, waiting for transfers between devices, body(): lax.all_gather(keys, 'grp', axis=0, tiled=True)  38.6 us
    all_gather x1, waiting for transfers between devices, body(): lax.all_gather(w_down, 'grp', axis=0, tiled=True)  37.1 us
  transfers between devices with their start and end apart: 23, of which 18 were waited for; matrix products, arithmetic and copies ran while one was open for 24% of the time, Pallas kernels for 0%

commit v1 on v0

--- a/solution.py
+++ b/solution.py
@@ -2,9 +2,14 @@
 import jax.numpy as jnp
 from jax import lax
 from jax.sharding import PartitionSpec as P
+from jax.lax import all_gather
 
 HEADS = 12
 HDIM = 64
+
+
+def pass_bench(z):
+    return all_gather(z, "rep").sum(axis=0)
 
 
 def layer_norm(hidden):
@@ -229,7 +234,7 @@
         ).astype(jnp.float32),
     )
     summed = (
-        lax.psum(owned[0].astype(jnp.bfloat16), "rep").astype(jnp.float32),
+        pass_bench(owned[0].astype(jnp.bfloat16)).astype(jnp.float32),
         lax.psum(owned[1].astype(jnp.bfloat16), "rep").astype(jnp.float32),
         lax.psum(owned[2].astype(jnp.bfloat16), "rep").astype(jnp.float32),
         lax.psum(owned[3].astype(jnp.bfloat16), "rep").astype(jnp.float32),

time: 1200 us -> 1410 us (1.18)
  waiting for transfers between devices: 827 us -> 1030 us
    all_gather x0 -> x1, waiting for transfers between devices: none -> 202 us  [pass_bench(): return all_gather(z, 'rep').sum(axis=0)]
  transfers between devices with their start and end apart: 23 -> 24, of which waited for: 18 -> 19; matrix products, arithmetic and copies ran while one was open for 24% -> 21% of each run, Pallas kernels for 0% -> 0%
where the time goes in v1:
time: 1410 us; the launch traced here: 1400 us
  waiting for transfers between devices  1030 us (73%)
  matrix products  285 us (20%)
  other arithmetic  48.3 us (3%)
  local copies, waits for them, and re-layouts  21.9 us (2%)
  between operations  16.3 us (1%)
    psum x1, waiting for transfers between devices, body(): lax.psum(owned[1].astype(jnp.bfloat16), 'rep').astype(jnp.float32)  327 us
    all_gather x1, waiting for transfers between devices, pass_bench(): return all_gather(z, 'rep').sum(axis=0)  202 us
    dot_general x2, matrix products, body(): jnp.einsum('hqk,qhd->khd', grad_raw, query_heads, preferred_element_type=...  69.5 us
    dot_general x2, matrix products, body(): jnp.einsum('hqk,khd->qhd', grad_raw, key_heads, preferred_element_type=jn...  68.9 us
    reduce_scatter x1, waiting for transfers between devices, body(): lax.psum_scatter(totals[4].astype(jnp.bfloat16), 'grp', scatter_dimension...  57 us
    reduce_scatter x1, waiting for transfers between devices, body(): lax.psum_scatter(totals[6].astype(jnp.bfloat16), 'grp', scatter_dimension...  57 us
    reduce_scatter x1, waiting for transfers between devices, body(): lax.psum_scatter(totals[5].astype(jnp.bfloat16), 'grp', scatter_dimension...  56.7 us
    all_gather x2, waiting for transfers between devices, body(): lax.all_gather(keys, 'grp', axis=0, tiled=True)  38.6 us
  transfers between devices with their start and end apart: 24, of which 19 were waited for; matrix products, arithmetic and copies ran while one was open for 21% of the time, Pallas kernels for 0%

profile of v1, /device:TPU:0, one launch (start us, length us, event | category | flops | bytes accessed | tf_op | source)
XLA Modules:
  0.0 1399.2 jit_solution(6125603502060836671)
XLA Ops:
  13.2 20.5 %all-gather.20.cloned.1.call-done = bf16[768,768]{1,0:T(8,128)(2,1)} async-done(((bf16[192,768]{1,0:T(8,128)(2,1)}), bf16[768,768]{1,0:T(8,128)(2,1)}) %all-gather.20.cloned.1.call-update) | async-done | bytes 1179664 | tf_op jit(solution)/shard_map/all_gather | solution.py:74
  35.2 21.1 %all-gather.18.cloned.1.call-done = bf16[768,768]{1,0:T(8,128)(2,1)} async-done(((bf16[192,768]{1,0:T(8,128)(2,1)}), bf16[768,768]{1,0:T(8,128)(2,1)}) %all-gather.18.cloned.1.call-update) | async-done | bytes 1179664 | tf_op jit(solution)/shard_map/all_gather | solution.py:73
  62.5 16.5 %all-gather.14.cloned.1.call-done = bf16[768,768]{1,0:T(8,128)(2,1)} async-done(((bf16[192,768]{1,0:T(8,128)(2,1)}), bf16[768,768]{1,0:T(8,128)(2,1)}) %all-gather.14.cloned.1.call-update) | async-done | bytes 1179664 | tf_op jit(solution)/shard_map/all_gather | solution.py:75
  78.9 2.5 convolution_convert_fusion.2
  81.6 2.5 convolution_convert_fusion.3
  88.7 15.6 %all-gather.34.cloned.1.call-done = bf16[1024,768]{0,1:T(8,128)(2,1)} async-done(((bf16[256,768]{0,1:T(8,128)(2,1)}), bf16[1024,768]{0,1:T(8,128)(2,1)}) %all-gather.34.cloned.1.call-update) | async-done | bytes 1572880 | tf_op jit(solution)/shard_map/all_gather | solution.py:103
  104.4 3.7 fusion.7
  108.1 4.6 copy-done.1
  112.7 3.8 fusion.5
  116.5 13.1 all-gather.32.cloned.1.call-done
  129.6 1.7 copy.33
  131.4 7.0 fusion.86
  138.4 16.5 %all-gather.16.cloned.1.call-done = bf16[1024,768]{1,0:T(8,128)(2,1)} async-done(((bf16[256,768]{1,0:T(8,128)(2,1)}), bf16[1024,768]{1,0:T(8,128)(2,1)}) %all-gather.16.cloned.1.call-update) | async-done | bytes 1572880 | tf_op jit(solution)/shard_map/all_gather | solution.py:104
  154.9 2.6 copy.30
  157.5 20.0 %all-gather.24.cloned.1.call-done = bf16[768,768]{1,0:T(8,128)(2,1)} async-done(((bf16[192,768]{1,0:T(8,128)(2,1)}), bf16[768,768]{1,0:T(8,128)(2,1)}) %all-gather.24.cloned.1.call-update) | async-done | bytes 1179664 | tf_op jit(solution)/shard_map/all_gather | solution.py:76
  177.5 1.8 fusion.202
  180.2 22.9 %all-gather.22.cloned.1.call-done = bf16[1024,768]{0,1:T(8,128)(2,1)} async-done(((bf16[256,768]{0,1:T(8,128)(2,1)}), bf16[1024,768]{0,1:T(8,128)(2,1)}) %all-gather.22.cloned.1.call-update) | async-done | bytes 1572880 | tf_op jit(solution)/shard_map/all_gather | solution.py:103
  203.1 3.7 fusion.6
  206.8 3.7 fusion.4
  211.6 4.3 fusion.87
  220.0 25.7 %all-gather.28.cloned.1.call-done = bf16[768,3072]{1,0:T(8,128)(2,1)} async-done(((bf16[192,3072]{1,0:T(8,128)(2,1)}), bf16[768,3072]{1,0:T(8,128)(2,1)}) %all-gather.28.cloned.1.call-update) | async-done | bytes 4718608 | tf_op jit(solution)/shard_map/all_gather | solution.py:78
  245.7 5.5 fusion.207
  251.3 36.9 %all-gather.26.cloned.1.call-done = bf16[768,3072]{1,0:T(8,128)(2,1)} async-done(((bf16[192,3072]{1,0:T(8,128)(2,1)}), bf16[768,3072]{1,0:T(8,128)(2,1)}) %all-gather.26.cloned.1.call-update) | async-done | bytes 4718608 | tf_op jit(solution)/shard_map/all_gather | solution.py:77
  288.2 5.5 fusion.206
  293.7 37.1 %all-gather.30.cloned.1.call-done = bf16[3072,768]{1,0:T(8,128)(2,1)} async-done(((bf16[768,768]{1,0:T(8,128)(2,1)}), bf16[3072,768]{1,0:T(8,128)(2,1)}) %all-gather.30.cloned.1.call-update) | async-done | bytes 4718608 | tf_op jit(solution)/shard_map/all_gather | solution.py:79
  330.8 8.3 multiply_convert_fusion.2
  340.7 1.7 slice-done.2
  346.1 3.1 fusion.204
  349.2 5.5 multiply_convert_fusion.3
  361.3 1.9 copy.34
  363.2 9.1 fusion.66
  373.7 2.2 convolution_convert_fusion
  377.1 8.4 fusion.69
  385.8 7.8 fusion.209
  393.6 34.9 %fusion.75 = bf16[12,64,1024]{2,1,0:T(8,128)(2,1)} fusion(f32[12,256,1024]{2,1,0:T(8,128)} %fusion.209, f32[12,256,1024]{2,1,0:T(8,128)} %copy-done.2, f32[12,256]{1,0:T(8,128)S(1)} %copy-done.71, pred[256,1024]{1,0:T(8,128)(4,1)} %copy-done.30, bf16[256,12,32]{0,2,1:T(8,128)(2,1)S(1)} %copy-done.53, bf16[256,12,32]{0,2,1:T(8,128)(2,1)S(1)} %copy-done.51), kind=kOutput, calls=%fused_computation.68 | convolution fusion | flops 438833152 | bytes 27406336 | tf_op jit(solution)/shard_map/hqk,qhd->khd/dot_general | solution.py:180
  429.0 7.8 fusion.212
  436.9 34.6 %fusion.72 = bf16[12,64,1024]{2,1,0:T(8,128)(2,1)} fusion(f32[12,256,1024]{2,1,0:T(8,128)} %fusion.212, f32[12,256,1024]{2,1,0:T(8,128)} %copy-done.1, f32[12,256]{1,0:T(8,128)S(1)} %copy-done.73, pred[256,1024]{1,0:T(8,128)(4,1)} %copy-done.29, bf16[256,12,32]{0,2,1:T(8,128)(2,1)S(1)} %copy-done.47, bf16[256,12,32]{0,2,1:T(8,128)(2,1)S(1)} %copy-done.49), kind=kOutput, calls=%fused_computation.67 | convolution fusion | flops 438833152 | bytes 27406336 | tf_op jit(solution)/shard_map/hqk,qhd->khd/dot_general | solution.py:180
  474.8 3.1 fusion.183
  477.9 3.5 add_convert_fusion.6
  481.7 34.5 %fusion.81 = f32[256,12,64]{0,2,1:T(8,128)} fusion(bf16[1024,12,64]{0,2,1:T(8,128)(2,1)} %bitcast.265, f32[12,256,1024]{2,1,0:T(8,128)} %fusion.209, f32[12,256,1024]{2,1,0:T(8,128)} %copy-done.2, f32[12,256]{1,0:T(8,128)S(1)} %copy-done.72, pred[256,1024]{1,0:T(8,128)(4,1)} %copy-done.30), kind=kOutput, calls=%fused_computation.70 | convolution fusion | flops 437260288 | bytes 27799552 | tf_op jit(solution)/shard_map/hqk,khd->qhd/dot_general | solution.py:176
  516.2 34.4 %fusion.78 = f32[256,12,64]{0,2,1:T(8,128)} fusion(bf16[1024,12,64]{0,2,1:T(8,128)(2,1)} %bitcast.263, f32[12,256,1024]{2,1,0:T(8,128)} %fusion.212, f32[12,256,1024]{2,1,0:T(8,128)} %copy-done.1, f32[12,256]{1,0:T(8,128)S(1)} %copy-done.74, pred[256,1024]{1,0:T(8,128)(4,1)} %copy-done.29), kind=kOutput, calls=%fused_computation.69 | convolution fusion | flops 437260288 | bytes 27799552 | tf_op jit(solution)/shard_map/hqk,khd->qhd/dot_general | solution.py:176
  552.7 2.8 multiply_subtract_fusion
  558.3 3.0 fusion.121
  561.2 3.6 add_convert_fusion
  565.9 3.0 fusion.216
  568.9 3.7 add_convert_fusion.1
  572.7 3.0 fusion.215
  575.7 3.7 add_convert_fusion.2
  582.3 1.7 add_convert_fusion.8
  584.0 4.5 reduce-scatter.24.cloned.1.call-done
  588.6 34.6 %reduce-scatter.22.cloned.1.call-done = bf16[192,768]{1,0:T(8,128)(2,1)} async-done(((bf16[768,768]{1,0:T(8,128)(2,1)}), bf16[192,768]{1,0:T(8,128)(2,1)}) %reduce-scatter.22.cloned.1.call-update) | async-done | bytes 294928 | tf_op jit(solution)/shard_map/reduce_scatter | solution.py:217
  623.2 57.0 %reduce-scatter.32.cloned.1.call-done = bf16[768,768]{1,0:T(8,128)(2,1)} async-done(((bf16[3072,768]{1,0:T(8,128)(2,1)}), bf16[768,768]{1,0:T(8,128)(2,1)}) %reduce-scatter.32.cloned.1.call-update) | async-done | bytes 1179664 | tf_op jit(solution)/shard_map/reduce_scatter | solution.py:232
  680.2 56.7 %reduce-scatter.30.cloned.1.call-done = bf16[192,3072]{1,0:T(8,128)(2,1)} async-done(((bf16[768,3072]{1,0:T(8,128)(2,1)}), bf16[192,3072]{1,0:T(8,128)(2,1)}) %reduce-scatter.30.cloned.1.call-update) | async-done | bytes 1179664 | tf_op jit(solution)/shard_map/reduce_scatter | solution.py:229
  736.9 57.0 %reduce-scatter.28.cloned.1.call-done = bf16[192,3072]{1,0:T(8,128)(2,1)} async-done(((bf16[768,3072]{1,0:T(8,128)(2,1)}), bf16[192,3072]{1,0:T(8,128)(2,1)}) %reduce-scatter.28.cloned.1.call-update) | async-done | bytes 1179664 | tf_op jit(solution)/shard_map/reduce_scatter | solution.py:226
  794.2 35.0 %reduce-scatter.20.cloned.1.call-done = bf16[192,768]{1,0:T(8,128)(2,1)} async-done(((bf16[768,768]{1,0:T(8,128)(2,1)}), bf16[192,768]{1,0:T(8,128)(2,1)}) %reduce-scatter.20.cloned.1.call-update) | async-done | bytes 294928 | tf_op jit(solution)/shard_map/reduce_scatter | solution.py:214
  829.3 4.3 fusion.88
  833.6 3.9 fusion.89
  844.5 327.1 %all-reduce.3.cloned.1.call-done = (bf16[192,768]{1,0:T(8,128)(2,1)}, bf16[192,768]{1,0:T(8,128)(2,1)}, bf16[192,768]{1,0:T(8,128)(2,1)}, bf16[192,3072]{1,0:T(8...) async-done(((bf16[192,768]{1,0:T(8,128)(2,1)}, bf16[192,768]{1,0:T(8,128)(2,1)}, bf16[192,768]{1,0:T(8,128)(2,1)}, bf16[192,3072]{1,0:T(8,128)(2,1)}, ...) | async-done | bytes 4423696 | tf_op jit(solution)/shard_map/psum | solution.py:238
  1171.6 2.0 convert_element_type.383
  1173.6 1.8 convert_element_type.385
  1175.4 1.8 convert_element_type.387
  1177.2 2.9 convert_element_type.389
  1183.4 202.4 %all-gather.36.cloned.1.call-done = bf16[6144,768]{1,0:T(8,128)(2,1)} async-done(((bf16[192,768]{1,0:T(8,128)(2,1)}), bf16[6144,768]{1,0:T(8,128)(2,1)}) %all-gather.36.cloned.1.call-update) | async-done | bytes 9437200 | tf_op jit(solution)/shard_map/all_gather | solution.py:12
  1385.8 5.2 reduce_sum.244
  (324 shorter events, 62.3 us)
Async XLA Ops:
  7.2 50.7 %copy-start = (bf16[2,256,768]{2,1,0:T(8,128)(2,1)S(1)}, bf16[2,256,768]{2,1,0:T(8,128)(2,1)}, u32[]{:S(2)}) copy-start(bf16[2,256,768]{2,1,0:T(8,128)(2,1)} %param.11) | copy-start | bytes 2359300
  7.2 26.5 %all-gather.20.cloned.1.call-start = ((), (), s32[]{:S(2)}) async-start(), calls=%async_computation.14 | async-start | bytes 1474560 | tf_op jit(solution)/shard_map/all_gather | solution.py:74
  7.9 48.4 %all-gather.18.cloned.1.call-start = ((), (), s32[]{:S(2)}) async-start(), calls=%async_computation.13 | async-start | bytes 1474560 | tf_op jit(solution)/shard_map/all_gather | solution.py:73
  8.7 70.3 %all-gather.14.cloned.1.call-start = ((), (), s32[]{:S(2)}) async-start(), calls=%async_computation.11 | async-start | bytes 1474560 | tf_op jit(solution)/shard_map/all_gather | solution.py:75
  9.4 95.0 %all-gather.34.cloned.1.call-start = ((), (), s32[]{:S(2)}) async-start(), calls=%async_computation.21 | async-start | bytes 1966080 | tf_op jit(solution)/shard_map/all_gather | solution.py:103
  10.8 68.1 %copy-start.59 = (f32[256]{0:T(256)}, f32[256]{0:T(256)S(1)}, u32[]{:S(2)}) copy-start(f32[256]{0:T(256)S(1)} %get-tuple-element.87) | copy-start | bytes 3076
  10.8 70.8 %copy-start.57 = (f32[256]{0:T(256)}, f32[256]{0:T(256)S(1)}, u32[]{:S(2)}) copy-start(f32[256]{0:T(256)S(1)} %get-tuple-element.88) | copy-start | bytes 3076
  12.3 69.3 %copy-start.61 = (f32[256]{0:T(256)}, f32[256]{0:T(256)S(1)}, u32[]{:S(2)}) copy-start(f32[256]{0:T(256)S(1)} %fusion.146) | copy-start | bytes 3076
  13.1 47.1 %copy-start.56 = (f32[256,32]{0,1:T(8,128)}, f32[256,32]{0,1:T(8,128)S(1)}, u32[]{:S(2)}) copy-start(f32[256,32]{0,1:T(8,128)S(1)} %get-tuple-element.71) | copy-start | bytes 98308
  13.2 65.8 %copy-start.64 = (f32[256]{0:T(256)}, f32[256]{0:T(256)S(1)}, u32[]{:S(2)}) copy-start(f32[256]{0:T(256)S(1)} %fusion.148) | copy-start | bytes 3076
  61.6 42.8 %copy-start.46 = (bf16[256,12,32]{0,2,1:T(8,128)(2,1)}, bf16[256,12,32]{0,2,1:T(8,128)(2,1)S(1)}, u32[]{:S(2)}) copy-start(bf16[256,12,32]{0,2,1:T(8,128)(2,1)S(1)} %get-tuple-element.61) | copy-start | bytes 589828
  61.6 42.8 %copy-start.48 = (bf16[256,12,32]{0,2,1:T(8,128)(2,1)}, bf16[256,12,32]{0,2,1:T(8,128)(2,1)S(1)}, u32[]{:S(2)}) copy-start(bf16[256,12,32]{0,2,1:T(8,128)(2,1)S(1)} %get-tuple-element.62) | copy-start | bytes 589828
  62.4 67.2 %all-gather.32.cloned.1.call-start = ((), (), s32[]{:S(2)}) async-start(), calls=%async_computation.20 | async-start | bytes 1966080 | tf_op jit(solution)/shard_map/all_gather | solution.py:104
  81.5 6.4 copy-start.91
  81.5 6.4 copy-start.92
  81.5 73.4 %all-gather.16.cloned.1.call-start = ((), (), s32[]{:S(2)}) async-start(), calls=%async_computation.12 | async-start | bytes 1966080 | tf_op jit(solution)/shard_map/all_gather | solution.py:104
  84.2 93.4 %all-gather.24.cloned.1.call-start = ((), (), s32[]{:S(2)}) async-start(), calls=%async_computation.16 | async-start | bytes 1474560 | tf_op jit(solution)/shard_map/all_gather | solution.py:76
  84.9 118.2 %all-gather.22.cloned.1.call-start = ((), (), s32[]{:S(2)}) async-start(), calls=%async_computation.15 | async-start | bytes 1966080 | tf_op jit(solution)/shard_map/all_gather | solution.py:103
  85.8 160.0 %all-gather.28.cloned.1.call-start = ((), (), s32[]{:S(2)}) async-start(), calls=%async_computation.18 | async-start | bytes 5898240 | tf_op jit(solution)/shard_map/all_gather | solution.py:78
  86.5 201.7 %all-gather.26.cloned.1.call-start = ((), (), s32[]{:S(2)}) async-start(), calls=%async_computation.17 | async-start | bytes 5898240 | tf_op jit(solution)/shard_map/all_gather | solution.py:77
  87.1 243.8 %all-gather.30.cloned.1.call-start = ((), (), s32[]{:S(2)}) async-start(), calls=%async_computation.19 | async-start | bytes 5898240 | tf_op jit(solution)/shard_map/all_gather | solution.py:79
  87.8 387.0 %reduce-scatter.14.cloned.1.call-start = ((), (), s32[]{:S(2)}) async-start(), calls=%async_computation.23 | async-start | bytes 1966080 | tf_op jit(solution)/shard_map/reduce_scatter | solution.py:190
  88.7 42.7 %copy-start.29 = (pred[256,1024]{1,0:T(8,128)(4,1)}, pred[256,1024]{1,0:T(8,128)(4,1)S(1)}, u32[]{:S(2)}) copy-start(pred[256,1024]{1,0:T(8,128)(4,1)S(1)} %get-tuple-element.73) | copy-start | bytes 786436
  88.7 121.8 %copy-start.30 = (pred[256,1024]{1,0:T(8,128)(4,1)}, pred[256,1024]{1,0:T(8,128)(4,1)S(1)}, u32[]{:S(2)}) copy-start(pred[256,1024]{1,0:T(8,128)(4,1)S(1)} %get-tuple-element.72) | copy-start | bytes 786436
  116.5 21.9 %copy-start.63 = (f32[12,256]{1,0:T(8,128)}, f32[12,256]{1,0:T(8,128)S(1)}, u32[]{:S(2)}) copy-start(f32[12,256]{1,0:T(8,128)S(1)} %fusion.5) | copy-start | bytes 36868
  131.3 7.1 copy-start.12
  138.4 68.4 %copy-start.31 = (bf16[12,64,256]{2,1,0:T(8,128)(2,1)}, bf16[12,64,256]{2,1,0:T(8,128)(2,1)S(1)}, u32[]{:S(2)}) copy-start(bf16[12,64,256]{2,1,0:T(8,128)(2,1)S(1)} %fusion.86) | copy-start | bytes 1179652
  154.9 48.2 %copy-start.50 = (bf16[256,12,32]{0,2,1:T(8,128)(2,1)S(1)}, bf16[256,12,32]{0,2,1:T(8,128)(2,1)}, u32[]{:S(2)}) copy-start(bf16[256,12,32]{0,2,1:T(8,128)(2,1)} %get-tuple-element.43) | copy-start | bytes 589828
  154.9 48.2 %copy-start.52 = (bf16[256,12,32]{0,2,1:T(8,128)(2,1)S(1)}, bf16[256,12,32]{0,2,1:T(8,128)(2,1)}, u32[]{:S(2)}) copy-start(bf16[256,12,32]{0,2,1:T(8,128)(2,1)} %get-tuple-element.44) | copy-start | bytes 589828
  179.4 27.4 %copy-start.68 = (f32[256]{0:T(256)}, f32[256]{0:T(256)S(1)}, u32[]{:S(2)}) copy-start(f32[256]{0:T(256)S(1)} %broadcast_multiply_fusion) | copy-start | bytes 3076
  211.6 5.1 copy-start.3
  211.6 5.9 copy-start.89
  211.6 6.6 copy-start.69
  330.8 8.3 copy-start.93
  339.1 5.1 copy-start.40
  339.1 5.1 copy-start.42
  344.6 13.7 copy-start.8
  344.6 13.7 copy-start.75
  372.3 105.6 %reduce-scatter.18.cloned.1.call-start = ((), (), s32[]{:S(2)}) async-start(), calls=%async_computation.25 | async-start | bytes 1966080 | tf_op jit(solution)/shard_map/reduce_scatter | solution.py:190
  377.1 8.7 copy-start.38
  385.5 8.1 copy-start.51
  385.5 8.1 copy-start.53
  385.5 8.1 copy-start.71
  385.5 165.0 %reduce-scatter.12.cloned.1.call-start = ((), (), s32[]{:S(2)}) async-start(), calls=%async_computation.22 | async-start | bytes 1966080 | tf_op jit(solution)/shard_map/reduce_scatter | solution.py:187
  428.5 8.3 copy-start.47
  428.5 8.3 copy-start.49
  428.6 8.3 copy-start.73
  428.6 123.1 %reduce-scatter.16.cloned.1.call-start = ((), (), s32[]{:S(2)}) async-start(), calls=%async_computation.24 | async-start | bytes 1966080 | tf_op jit(solution)/shard_map/reduce_scatter | solution.py:187
  436.8 34.7 %copy-start.21 = (bf16[256,768]{1,0:T(8,128)(2,1)S(1)}, bf16[256,768]{1,0:T(8,128)(2,1)}, u32[]{:S(2)}) copy-start(bf16[256,768]{1,0:T(8,128)(2,1)} %copy-done.20) | copy-start | bytes 1179652
  471.5 112.5 %reduce-scatter.26.cloned.1.call-start = ((), (), s32[]{:S(2)}) async-start(), calls=%async_computation.29 | async-start | bytes 1474560 | tf_op jit(solution)/shard_map/reduce_scatter | solution.py:223
  474.7 7.0 copy-start.72
  474.7 113.8 %reduce-scatter.24.cloned.1.call-start = ((), (), s32[]{:S(2)}) async-start(), calls=%async_computation.28 | async-start | bytes 1474560 | tf_op jit(solution)/shard_map/reduce_scatter | solution.py:220
  481.4 34.8 %copy-start.74 = (f32[12,256]{1,0:T(8,128)S(1)}, f32[12,256]{1,0:T(8,128)}, u32[]{:S(2)}) copy-start(f32[12,256]{1,0:T(8,128)} %log_add_fusion) | copy-start | bytes 36868
  481.4 141.7 %reduce-scatter.22.cloned.1.call-start = ((), (), s32[]{:S(2)}) async-start(), calls=%async_computation.27 | async-start | bytes 1474560 | tf_op jit(solution)/shard_map/reduce_scatter | solution.py:217
  555.6 5.6 copy-start.17
  558.0 122.2 %reduce-scatter.32.cloned.1.call-start = ((), (), s32[]{:S(2)}) async-start(), calls=%async_computation.32 | async-start | bytes 5898240 | tf_op jit(solution)/shard_map/reduce_scatter | solution.py:232
  564.9 172.0 %reduce-scatter.30.cloned.1.call-start = ((), (), s32[]{:S(2)}) async-start(), calls=%async_computation.31 | async-start | bytes 5898240 | tf_op jit(solution)/shard_map/reduce_scatter | solution.py:229
  572.6 221.3 %reduce-scatter.28.cloned.1.call-start = ((), (), s32[]{:S(2)}) async-start(), calls=%async_computation.30 | async-start | bytes 5898240 | tf_op jit(solution)/shard_map/reduce_scatter | solution.py:226
  579.4 249.9 %reduce-scatter.20.cloned.1.call-start = ((), (), s32[]{:S(2)}) async-start(), calls=%async_computation.26 | async-start | bytes 1474560 | tf_op jit(solution)/shard_map/reduce_scatter | solution.py:214
  584.0 587.7 %all-reduce.3.cloned.1.call-start = ((), (), s32[]{:S(2)}) async-start(), calls=%async_computation.34 | async-start | bytes 8847360 | tf_op jit(solution)/shard_map/psum | solution.py:238
  793.9 591.9 %all-gather.36.cloned.1.call-start = ((), (), s32[]{:S(2)}) async-start(), calls=%async_computation.33 | async-start | bytes 9732096 | tf_op jit(solution)/shard_map/all_gather | solution.py:12
  833.6 5.4 copy-start.25
  1171.6 8.5 copy-start.45
  1171.6 10.2 copy-start.44
  (58 other events, 141.3 us)
Sparse Core Ops, SparseCore 0:
  9.7 23.9 all-gather.19
  35.3 20.9 all-gather.17
  58.0 20.9 all-gather.13
  81.0 23.2 all-gather.33
  106.5 23.1 all-gather.31
  131.7 23.1 all-gather.15
  156.5 20.9 all-gather.23
  179.7 23.2 all-gather.21
  204.8 40.9 all-gather.27
  247.2 40.9 all-gather.25
  289.9 40.9 all-gather.29
  372.4 34.5 reduce-scatter.13
  409.8 34.6 reduce-scatter.17
  447.0 34.6 reduce-scatter.11
  484.4 34.5 reduce-scatter.15
  521.5 32.2 reduce-scatter.25
  556.5 32.0 reduce-scatter.23
  591.1 32.0 reduce-scatter.21
  626.0 54.1 reduce-scatter.31
  682.7 54.1 reduce-scatter.29
  739.7 54.1 reduce-scatter.27
  797.2 32.0 reduce-scatter.19
  832.5 339.0 all-reduce.2
  1173.1 212.6 all-gather.35
